TPU v7x, 768 devices: a whole 4x8x12 slice. The times are simulated.
768 devices in a mesh: region: 2 (over core), island: 12 (over z_hi, x), dev: 32 (over z_lo, y).
Axes of the slice: x: 4, y: 8, z: 12 (z_hi: 3, z_lo: 4; z = z_hi * 4 + z_lo), core: 2. Of those that a mesh axis runs over, the one named last changes fastest.
Arguments:
- activations: bfloat16 [196608, 2560], P(('region', 'island', 'dev')), may hold values from -6 to 6
- cotangent: bfloat16 [196608, 512], P(('region', 'island', 'dev')), may hold values from -6 to 6
- island_weight: float32 [2, 12, 2560, 512], P('region', 'island', 'dev'), may hold values from -6 to 6
- adam_first: float32 [2, 12, 2560, 512], P('region', 'island', 'dev'), may hold values from -6 to 6
- adam_second: float32 [2, 12, 2560, 512], P('region', 'island', 'dev'), may hold values from 0.01 to 1
- region_anchor: float32 [2, 2560, 512], P('region', 'dev'), may hold values from -6 to 6
- region_momentum: float32 [2, 2560, 512], P('region', 'dev'), may hold values from -6 to 6
- global_anchor: float32 [2560, 512], P('dev'), may hold values from -6 to 6
- global_momentum: float32 [2560, 512], P('dev'), may hold values from -6 to 6
Outputs:
- first_new: float32 [2, 12, 2560, 512], P('region', 'island', 'dev')
- second_new: float32 [2, 12, 2560, 512], P('region', 'island', 'dev')
- region_velocity: float32 [2, 2560, 512], P('region', 'dev')
- global_velocity: float32 [2560, 512], P('dev')
- global_new: float32 [2560, 512], P('dev')
- next_keys: bfloat16 [196608, 512], P(('region', 'island', 'dev'))
All inputs are finite; a program needn't handle non-finite values.
Results may differ from a plain program's by a relative error of at most 0.0049.
Values may be sent and summed in bfloat16 or wider, within the bound.
A program may use at most 32 MiB of HBM per device.

v0:
```python
import math

import jax
import jax.numpy as jnp
from jax import lax
from jax.sharding import Mesh
from jax.sharding import PartitionSpec as P

DW = 2560
DEV = ("dev_0", "dev_1")
REGION_ISLAND_DEV = ("region", "island", "dev_0", "dev_1")


beta_first = 0.9
beta_second = 0.999
adam_eps = 1e-08
inner_rate = 0.05
weight_decay = 0.1
region_mu = 0.9
region_rate = 0.7
global_mu = 0.9
global_rate = 0.7


def reduced_to_own(pieces, axes, turns):
    dims = [lax.axis_size(a) for a in axes]
    pieces = pieces.reshape(*dims, *pieces.shape[1:])
    pieces = pieces.transpose(*turns, *range(len(axes), pieces.ndim))
    pieces = pieces.reshape(-1, *pieces.shape[len(axes) :])
    for k in turns:
        pieces = lax.psum_scatter(pieces, axes[k], scatter_dimension=0, tiled=True)
    return pieces[0]


def in_blocks(shard, dim, length):
    before, after = (shard.shape[:dim], shard.shape[dim + 1 :])
    return jnp.moveaxis(shard.reshape(*before, length, -1, *after), dim, 0)


def summed_rows_2(shard, axes, turns, dim):
    length = lax.axis_size(axes)
    return reduced_to_own(in_blocks(shard, dim, length), axes, turns)


def over_pieces(shard, axis):
    return lax.all_gather(shard, axis).sum(0)


def copy_for_each(shard, axis):
    copies = jnp.broadcast_to(shard, (lax.axis_size(axis), *shard.shape))
    return lax.all_to_all(copies, axis, split_axis=0, concat_axis=0, tiled=True)


def over_copies(shard, axis):
    return copy_for_each(shard, axis).sum(axis=0)


def in_order(pieces, dim):
    pieces = jnp.moveaxis(pieces, 0, dim)
    dims = pieces.shape
    return pieces.reshape(*dims[:dim], dims[dim] * dims[dim + 1], *dims[dim + 2 :])


def gathered_copies(shard, axis, dim):
    pieces = copy_for_each(shard, axis)
    return in_order(pieces, dim)


def body(
    activations,
    cotangent,
    island_weight,
    adam_first,
    adam_second,
    region_anchor,
    region_momentum,
    global_anchor,
    global_momentum,
):
    island_tokens = activations.shape[0] * lax.axis_size(DEV)
    islands = lax.axis_size("island")
    regions = lax.axis_size("region")
    summed = summed_rows_2(
        lax.dot_general(
            activations, cotangent, (((0,), (0,)), ((), ())), preferred_element_type=jnp.float32
        ).astype(jnp.bfloat16),
        DEV,
        (1, 0),
        0,
    ).astype(jnp.float32)
    gradient = summed * (1.0 / math.sqrt(island_tokens))
    first_new = beta_first * adam_first + (1.0 - beta_first) * gradient
    second_new = beta_second * adam_second + (1.0 - beta_second) * gradient * gradient
    inner = island_weight - inner_rate * (
        first_new / (jnp.sqrt(second_new) + adam_eps) + weight_decay * island_weight
    )
    island_delta = region_anchor[:, None] - inner
    island_total = over_pieces(island_delta, "island")
    region_mean = island_total[:, 0] / islands
    region_velocity = region_mu * region_momentum + region_mean
    region_params = region_anchor - region_rate * (region_mean + region_mu * region_velocity)
    region_gap = global_anchor[None] - region_params
    gap_total = over_copies(region_gap, "region")
    global_mean = gap_total[0] / regions
    global_velocity = global_mu * global_momentum + global_mean
    global_new = global_anchor - global_rate * (global_mean + global_mu * global_velocity)
    weight_low = global_new.astype(jnp.bfloat16)
    weight_full = gathered_copies(weight_low, DEV, 0)
    projected = jnp.dot(activations, weight_full, preferred_element_type=jnp.float32)
    next_keys = (projected * (1.0 / math.sqrt(DW))).astype(jnp.bfloat16)
    return (first_new, second_new, region_velocity, global_velocity, global_new, next_keys)


def solution(mesh):
    finer = Mesh(
        mesh.devices.reshape(mesh.shape["region"], mesh.shape["island"], 4, 8),
        ("region", "island", "dev_0", "dev_1"),
    )
    placed = (
        P(REGION_ISLAND_DEV, None),
        P(REGION_ISLAND_DEV, None),
        P("region", "island", DEV, None),
        P("region", "island", DEV, None),
        P("region", "island", DEV, None),
        P("region", DEV, None),
        P("region", DEV, None),
        P(DEV, None),
        P(DEV, None),
    )
    return jax.shard_map(
        body,
        mesh=finer,
        in_specs=placed,
        out_specs=(
            P("region", "island", DEV, None),
            P("region", "island", DEV, None),
            P("region", DEV, None),
            P(DEV, None),
            P(DEV, None),
            P(REGION_ISLAND_DEV, None),
        ),
        check_vma=False,
    )
```

profile of v0, /device:TPU:1, one launch (start us, length us, event | category | flops | bytes accessed | tf_op | source)
XLA Modules:
  0.0 286.8 jit_solution(9290443420450824114)
XLA Ops:
  7.2 0.0 copy-start
  7.2 0.0 reduce-scatter.3.cloned.1.call-start
  7.2 1.3 copy-done
  8.5 1.8 convolution_convert_fusion
  10.3 1.7 copy.19
  12.0 0.0 copy-start.2
  12.0 0.0 copy-start.7
  12.0 0.0 reduce-scatter.3.cloned.1.call-update
  12.1 0.0 reduce-scatter.5.cloned.1.call-start
  12.1 53.1 %reduce-scatter.3.cloned.1.call-done = bf16[4,80,512]{2,1,0:T(8,128)(2,1)} async-done(((bf16[32,80,512]{2,1,0:T(8,128)(2,1)}), bf16[4,80,512]{2,1,0:T(8,128)(2,1)}) %reduce-scatter.3.cloned.1.call-update) | async-done | bytes 327696 | tf_op jit(solution)/shard_map/reduce_scatter | solution.py:31
  65.2 0.0 reduce-scatter.5.cloned.1.call-update
  65.2 0.0 all-gather.3.cloned.1.call-start
  65.3 35.7 %reduce-scatter.5.cloned.1.call-done = bf16[1,80,512]{2,1,0:T(8,128)(2,1)} async-done(((bf16[4,80,512]{2,1,0:T(8,128)(2,1)}), bf16[1,80,512]{2,1,0:T(8,128)(2,1)}) %reduce-scatter.5.cloned.1.call-update) | async-done | bytes 81936 | tf_op jit(solution)/shard_map/reduce_scatter | solution.py:31
  101.0 1.7 bitcast_subtract_fusion.1
  102.8 0.0 all-gather.3.cloned.1.call-update
  102.8 92.7 %all-gather.3.cloned.1.call-done = f32[12,1,80,512]{3,2,1,0:T(8,128)} async-done(((f32[1,1,80,512]{3,2,1,0:T(8,128)}), f32[12,1,80,512]{3,2,1,0:T(8,128)}) %all-gather.3.cloned.1.call-update) | async-done | bytes 1966096 | tf_op jit(solution)/shard_map/all_gather | solution.py:46
  195.5 1.7 reduce.2
  197.2 0.7 fusion.7
  198.0 5.0 %all_to_all.10 = f32[2,1,80,512]{3,2,1,0:T(8,128)S(1)} all-to-all(f32[2,1,80,512]{3,2,1,0:T(8,128)S(1)} %broadcast_in_dim.16), channel_id=1, replica_groups=mesh['region'=2,'island'=12,'dev_0'=4,'dev_1'=8] {'region'}, dimensions={0} | all-to-all | bytes 655360 | tf_op jit(solution)/shard_map/all_to_all | solution.py:51
  203.1 0.8 fusion.10
  203.8 0.3 broadcast_in_dim.17
  204.1 74.3 %all_to_all.11 = bf16[32,80,512]{2,1,0:T(8,128)(2,1)S(1)} all-to-all(bf16[32,80,512]{2,1,0:T(8,128)(2,1)S(1)} %broadcast_in_dim.17), channel_id=1, replica_groups=mesh['region'=2,'island'=12,'dev_0'=4,'dev_1'=8] {'dev_0','dev_1'}, dimensions={0} | all-to-all | bytes 5242880 | tf_op jit(solution)/shard_map/all_to_all | solution.py:51
  278.5 0.9 fusion.1
  279.4 0.8 copy.20
  (14 shorter events, 0.1 us)
Async XLA Ops:
  7.2 1.3 copy-start
  7.2 58.0 %reduce-scatter.3.cloned.1.call-start = ((), (), s32[]{:S(2)}) async-start(), calls=%async_computation.4 | async-start | bytes 2949120 | tf_op jit(solution)/shard_map/reduce_scatter | solution.py:31
  12.0 89.0 %copy-start.1 = (f32[1,80,512]{2,1,0:T(8,128)S(1)}, f32[1,80,512]{2,1,0:T(8,128)}, u32[]{:S(2)}) copy-start(f32[1,80,512]{2,1,0:T(8,128)} %param.14) | copy-start | bytes 491524
  12.0 89.0 %copy-start.3 = (f32[1,1,80,512]{3,2,1,0:T(8,128)S(1)}, f32[1,1,80,512]{3,2,1,0:T(8,128)}, u32[]{:S(2)}) copy-start(f32[1,1,80,512]{3,2,1,0:T(8,128)} %param.11) | copy-start | bytes 491524
  12.0 89.0 %copy-start.4 = (f32[1,1,80,512]{3,2,1,0:T(8,128)S(1)}, f32[1,1,80,512]{3,2,1,0:T(8,128)}, u32[]{:S(2)}) copy-start(f32[1,1,80,512]{3,2,1,0:T(8,128)} %param.13) | copy-start | bytes 491524
  12.0 89.0 %copy-start.5 = (f32[1,1,80,512]{3,2,1,0:T(8,128)S(1)}, f32[1,1,80,512]{3,2,1,0:T(8,128)}, u32[]{:S(2)}) copy-start(f32[1,1,80,512]{3,2,1,0:T(8,128)} %param.12) | copy-start | bytes 491524
  12.0 185.2 %copy-start.2 = (f32[80,512]{1,0:T(8,128)S(1)}, f32[80,512]{1,0:T(8,128)}, u32[]{:S(2)}) copy-start(f32[80,512]{1,0:T(8,128)} %param.16) | copy-start | bytes 491524
  12.0 185.2 %copy-start.7 = (f32[1,80,512]{2,1,0:T(8,128)S(1)}, f32[1,80,512]{2,1,0:T(8,128)}, u32[]{:S(2)}) copy-start(f32[1,80,512]{2,1,0:T(8,128)} %param.15) | copy-start | bytes 491524
  12.1 89.0 %reduce-scatter.5.cloned.1.call-start = ((), (), s32[]{:S(2)}) async-start(), calls=%async_computation.5 | async-start | bytes 409600 | tf_op jit(solution)/shard_map/reduce_scatter | solution.py:31
  65.2 130.3 %all-gather.3.cloned.1.call-start = ((), (), s32[]{:S(2)}) async-start(), calls=%async_computation.6 | async-start | bytes 2129920 | tf_op jit(solution)/shard_map/all_gather | solution.py:46
  102.8 100.3 %copy-start.6 = (f32[80,512]{1,0:T(8,128)S(1)}, f32[80,512]{1,0:T(8,128)}, u32[]{:S(2)}) copy-start(f32[80,512]{1,0:T(8,128)} %param.17) | copy-start | bytes 491524
Sparse Core Ops, SparseCore 0:
  12.2 52.9 reduce-scatter.2
  68.3 32.6 reduce-scatter.4
  105.6 89.8 all-gather.2
where the time goes:
time: 288 us; the launch traced here: 287 us
  waiting for transfers between devices  182 us (63%)
  blocking collectives  79.4 us (28%)
  between operations  13.8 us (5%)
  other arithmetic  4.97 us (2%)
  local copies, waits for them, and re-layouts  4.14 us (1%)
    all_gather x1, waiting for transfers between devices, over_pieces(): return lax.all_gather(shard, axis).sum(0)  92.7 us
    reduce_scatter x2, waiting for transfers between devices, reduced_to_own(): pieces = lax.psum_scatter(pieces, axes[k], scatter_dimension=0, tiled=True)  88.8 us
    all_to_all x2, blocking collectives, copy_for_each(): return lax.all_to_all(copies, axis, split_axis=0, concat_axis=0, tiled=True)  79.4 us
  transfers between devices with their start and end apart: 3, of which 3 were waited for; matrix products, arithmetic and copies ran while one was open for 0% of the time, Pallas kernels for 0%

commit v1 on v0

v1 whole, which is shorter than its diff:
```python
import functools
import math

import jax
import jax.numpy as jnp
from jax import lax
from jax.experimental import pallas as pl
from jax.experimental.pallas import tpu as pltpu
from jax.sharding import Mesh
from jax.sharding import PartitionSpec as P

DW = 2560
KV = 512
TOK = 256
ROWS = 80
LB = 128
N_Y = 8
N_ZL = 4
N_ZH = 3
N_X = 4
MESH = pl.DeviceIdType.MESH
BF = jnp.bfloat16
F32 = jnp.float32

beta_first = 0.9
beta_second = 0.999
adam_eps = 1e-08
inner_rate = 0.05
weight_decay = 0.1
region_mu = 0.9
region_rate = 0.7
global_mu = 0.9
global_rate = 0.7

W_, M_, V_, RA, RM, GA, GM = range(7)
O_FIRST, O_SECOND, O_RV, O_GV, O_GN = range(5)
SIGN = (1, -1)


def hops(d, lb):
    return 4 if (lb % 2 == 0) == (d == 0) else 3


def kernel(
    act_hbm, cot_hbm, w_hbm, m_hbm, v_hbm, ra_hbm, rm_hbm, ga_hbm, gm_hbm,
    of_hbm, os_hbm, orv_hbm, ogv_hbm, ogn_hbm, okeys_hbm,
    act, cot, state, part, yrec, ysum, zrec, zfar, ypart, yfar, delta, xrec, trec,
    gap, means, wfull, ksend, krec, outs, keys,
    in_sem, out_sem, act_sem, ys_sem, yr_sem, zs_sem, zr_sem, fs_sem, fr_sem,
    xs_sem, xr_sem, ts_sem, tr_sem, g_sem, ms_sem, mr_sem, wxs_sem, wxr_sem,
    wzs_sem, wzr_sem, wys_sem, wyr_sem, k_sem,
):
    r = lax.axis_index("region")
    zh = lax.axis_index("zh")
    x = lax.axis_index("x")
    zl = lax.axis_index("zl")
    y = lax.axis_index("y")
    z = zh * 4 + zl
    other = {"region": 1 - r}

    def to_z(off):
        t = lax.rem(z + off + 12, 12)
        return {"zh": t // 4, "zl": lax.rem(t, 4)}

    def to_y(off):
        return {"y": lax.rem(y + off + N_Y, N_Y)}

    def to_x(off):
        return {"x": lax.rem(x + off + N_X, N_X)}

    def remote(src, dst, ssem, rsem, dev):
        return pltpu.make_async_remote_copy(
            src_ref=src, dst_ref=dst, send_sem=ssem, recv_sem=rsem,
            device_id=dev, device_id_type=MESH,
        )

    drains = []

    def go(c):
        c.start()
        drains.append(c.wait_send)

    def go_if(cond, make):
        @pl.when(cond)
        def _():
            make().start()

        def drain():
            @pl.when(cond)
            def _():
                make().wait_send()

        drains.append(drain)

    loads = [
        pltpu.make_async_copy(act_hbm, act.at[0], in_sem.at[0]),
        pltpu.make_async_copy(cot_hbm, cot, in_sem.at[1]),
    ]
    for i, ref in enumerate((w_hbm, m_hbm, v_hbm, ra_hbm, rm_hbm, ga_hbm, gm_hbm)):
        loads.append(pltpu.make_async_copy(ref, state.at[i], in_sem.at[2 + i]))
    for c in loads:
        c.start()
    stores = [
        pltpu.make_async_copy(outs.at[i], o, out_sem.at[i])
        for i, o in enumerate((of_hbm, os_hbm, orv_hbm, ogv_hbm, ogn_hbm))
    ]

    barrier = pltpu.get_barrier_semaphore()
    peers = [other] + [to_y(k) for k in (1, -1)] + [to_x(k) for k in (1, 2, 3)]
    peers += [to_z(k) for k in (-4, -3, -2, -1, 1, 2, 3, 4)]
    for dev in peers:
        pl.semaphore_signal(barrier, inc=1, device_id=dev, device_id_type=MESH)

    loads[0].wait()
    loads[1].wait()

    def ysend(d, lb, s):
        t = lax.rem(y + SIGN[d] * (hops(d, lb) - s) + N_Y, N_Y)
        if lb == 3:
            src = ypart.at[t] if s == 0 else yfar.at[d, s - 1]
            dst = yfar.at[d, s]
        else:
            src = part.at[lb, t] if s == 0 else yrec.at[d, lb, s - 1]
            dst = yrec.at[d, lb, s]
        return remote(
            src, dst, ys_sem.at[d, lb, s], yr_sem.at[d, lb, s], to_y(SIGN[d])
        )

    def ystart(lb):
        for d in range(2):
            go(ysend(d, lb, 0))

    def ystep(lb, s):
        for d in range(2):
            n = hops(d, lb)
            if s >= n:
                continue
            ysend(d, lb, s).wait_recv()
            if s < n - 1:
                t = lax.rem(y + SIGN[d] * (n - s - 1) + N_Y, N_Y)
                if lb == 3:
                    yfar[d, s] = (
                        yfar[d, s].astype(F32) + ypart[t].astype(F32)
                    ).astype(BF)
                else:
                    yrec[d, lb, s] = (
                        yrec[d, lb, s].astype(F32) + part[lb, t].astype(F32)
                    ).astype(BF)
                go(ysend(d, lb, s + 1))

    def zsend(lb, k):
        t = lax.rem(zl + k, N_ZL)
        return remote(
            ysum.at[lb, t], zrec.at[lb, zl], zs_sem.at[lb, k - 1],
            zr_sem.at[lb, k - 1], {"zl": t},
        )

    def zrecv(lb, k):
        src = lax.rem(zl + N_ZL - k, N_ZL)
        return remote(
            ysum.at[lb, zl], zrec.at[lb, src], zs_sem.at[lb, k - 1],
            zr_sem.at[lb, k - 1], {"zl": src},
        )

    def yfinal(lb):
        total = (
            part[lb, y].astype(F32)
            + yrec[0, lb, hops(0, lb) - 1].astype(F32)
            + yrec[1, lb, hops(1, lb) - 1].astype(F32)
        )
        ysum[lb] = total.astype(BF)
        for k in (1, 2, 3):
            go(zsend(lb, k))

    def fsend(k):
        t = lax.rem(zl + k, N_ZL)
        return remote(
            part.at[3, :, t], zfar.at[k - 1], fs_sem.at[k - 1], fr_sem.at[k - 1],
            {"zl": t},
        )

    def far():
        for k in (1, 2, 3):
            fsend(k).wait_recv()
        for t in range(N_Y):
            total = part[3, t, zl].astype(F32)
            for k in range(3):
                total = total + zfar[k, t].astype(F32)
            ypart[t] = total.astype(BF)
        ystart(3)

    def xsend(lb):
        return remote(
            delta.at[lb], xrec.at[x], xs_sem.at[lb], xr_sem.at[x], {"x": lb}
        )

    def adam(lb):
        if lb == 3:
            g = (
                ypart[y].astype(F32)
                + yfar[0, hops(0, 3) - 1].astype(F32)
                + yfar[1, hops(1, 3) - 1].astype(F32)
            )
        else:
            for k in (1, 2, 3):
                zrecv(lb, k).wait_recv()
            g = ysum[lb, zl].astype(F32)
            for k in (1, 2, 3):
                g = g + zrec[lb, lax.rem(zl + k, N_ZL)].astype(F32)
        lanes = slice(lb * LB, (lb + 1) * LB)
        gradient = g * (1.0 / math.sqrt(TOK * 32))
        first = beta_first * state[M_, :, lanes] + (1.0 - beta_first) * gradient
        second = (
            beta_second * state[V_, :, lanes]
            + (1.0 - beta_second) * gradient * gradient
        )
        weight = state[W_, :, lanes]
        inner = weight - inner_rate * (
            first / (jnp.sqrt(second) + adam_eps) + weight_decay * weight
        )
        outs[O_FIRST, :, lanes] = first
        outs[O_SECOND, :, lanes] = second
        delta[lb] = (state[RA, :, lanes] - inner).astype(BF)
        go_if(x != lb, lambda: xsend(lb))

    mine = pl.ds(pl.multiple_of(x * LB, LB), LB)

    def tsend(k):
        return remote(
            trec.at[zh], trec.at[zh], ts_sem.at[k - 1], tr_sem.at[k - 1],
            {"zh": lax.rem(zh + k, N_ZH)},
        )

    def trecv(k):
        src = lax.rem(zh + N_ZH - k, N_ZH)
        return remote(
            trec.at[zh], trec.at[src], ts_sem.at[k - 1], tr_sem.at[k - 1], {"zh": src}
        )

    def gsend():
        return remote(gap.at[r], gap.at[r], g_sem.at[0], g_sem.at[1], other)

    def owner_a(h):
        @pl.when(x // 2 == h)
        def _():
            t = delta[x].astype(F32)
            for k in (1, 2, 3):
                src = lax.rem(x + k, N_X)
                remote(
                    delta.at[0], xrec.at[src], xs_sem.at[0], xr_sem.at[src], {"x": src}
                ).wait_recv()
                t = t + xrec[src].astype(F32)
            trec[zh] = t
            for k in (1, 2):
                tsend(k).start()

    def owner_b(h):
        @pl.when(x // 2 == h)
        def _():
            for k in (1, 2):
                trecv(k).wait_recv()
            region_mean = ((trec[0] + trec[1]) + trec[2]) / 12
            region_velocity = region_mu * state[RM, :, mine] + region_mean
            region_params = state[RA, :, mine] - region_rate * (
                region_mean + region_mu * region_velocity
            )
            gap[r] = state[GA, :, mine] - region_params
            gsend().start()
            means[x, 0] = region_mean

    def wxsend(h, k):
        slot = wfull.at[h, zl, y]
        return remote(slot, slot, wxs_sem.at[k - 1], wxr_sem.at[h], to_x(k))

    def msend(k):
        return remote(
            means.at[x], means.at[x], ms_sem.at[k - 1], mr_sem.at[x], to_x(k)
        )

    def owner_c(h):
        @pl.when(x // 2 == h)
        def _():
            remote(
                gap.at[r], gap.at[1 - r], g_sem.at[0], g_sem.at[1], other
            ).wait_recv()
            global_mean = (gap[0] + gap[1]) / 2
            global_velocity = global_mu * state[GM, :, mine] + global_mean
            global_new = state[GA, :, mine] - global_rate * (
                global_mean + global_mu * global_velocity
            )

            @pl.when(lax.rem(x, 2) == r)
            def _():
                wfull[h, zl, y] = global_new.astype(BF)
                for k in (1, 2, 3):
                    wxsend(h, k).start()

            means[x, 1] = global_mean
            for k in (1, 2, 3):
                msend(k).start()

    def wz_offs(h):
        return (1, -1, 2 if h == 0 else -2)

    def wzsend(h, i):
        slot = wfull.at[h, zl, y]
        return remote(
            slot, slot, wzs_sem.at[h, i], wzr_sem.at[h, i], to_z(wz_offs(h)[i])
        )

    def wzrecv(h, i):
        slot = wfull.at[h, lax.rem(zl - wz_offs(h)[i] + 4, 4), y]
        return remote(
            slot, slot, wzs_sem.at[h, i], wzr_sem.at[h, i], to_z(-wz_offs(h)[i])
        )

    def wz(h):
        @pl.when(x != 2 * h + r)
        def _():
            slot = wfull.at[h, zl, y]
            remote(
                slot, slot, wxs_sem.at[0], wxr_sem.at[h], {"x": 2 * h + r}
            ).wait_recv()

        for i in range(3):
            go(wzsend(h, i))

    def wysend(d, h, s):
        slot = wfull.at[h, :, lax.rem(y - SIGN[d] * s + N_Y, N_Y)]
        return remote(
            slot, slot, wys_sem.at[d, h, s], wyr_sem.at[d, h, s], to_y(SIGN[d])
        )

    def wyrecv(d, h, s):
        slot = wfull.at[h, :, lax.rem(y - SIGN[d] * (s + 1) + N_Y, N_Y)]
        return remote(
            slot, slot, wys_sem.at[d, h, s], wyr_sem.at[d, h, s], to_y(-SIGN[d])
        )

    def wystart(h):
        for i in range(3):
            wzrecv(h, i).wait_recv()
        for d in range(2):
            go(wysend(d, h, 0))

    def wystep(h, s):
        for d in range(2):
            n = hops(d, h)
            if s >= n:
                continue
            wyrecv(d, h, s).wait_recv()
            if s + 1 < n:
                go(wysend(d, h, s + 1))

    def replicated():
        for lb in range(4):
            @pl.when(x != lb)
            def _():
                remote(
                    means.at[x], means.at[lb], ms_sem.at[0], mr_sem.at[lb], {"x": lb}
                ).wait_recv()

            lanes = slice(lb * LB, (lb + 1) * LB)
            rmean = means[lb, 0]
            gmean = means[lb, 1]
            outs[O_RV, :, lanes] = region_mu * state[RM, :, lanes] + rmean
            gvel = global_mu * state[GM, :, lanes] + gmean
            outs[O_GV, :, lanes] = gvel
            outs[O_GN, :, lanes] = state[GA, :, lanes] - global_rate * (
                gmean + global_mu * gvel
            )
        for i in (O_RV, O_GV, O_GN):
            stores[i].start()
            drains.append(stores[i].wait)

    scale = 1.0 / math.sqrt(DW)

    def kcopy(h):
        return remote(ksend.at[h], krec.at[h], k_sem.at[h], k_sem.at[2 + h], other)

    def project(h):
        rhs = wfull[h].reshape(DW, LB)
        ksend[h] = (
            jnp.dot(act[1], rhs, preferred_element_type=F32) * scale
        ).astype(BF)
        go(kcopy(h))
        keys[:, pl.ds(pl.multiple_of((2 * h + r) * LB, LB), LB)] = (
            jnp.dot(act[0], rhs, preferred_element_type=F32) * scale
        ).astype(BF)

    act_copy = remote(act.at[0], act.at[1], act_sem.at[0], act_sem.at[1], other)
    for h in (1, 0):
        rhs = cot[:, h * 256 : (h + 1) * 256]
        for q in range(N_ZL):
            lhs = act[0, :, q * 640 : (q + 1) * 640]
            term = lax.dot_general(
                lhs, rhs, (((0,), (0,)), ((), ())), preferred_element_type=F32
            ).astype(BF)
            for b in range(2):
                for t in range(N_Y):
                    part[2 * h + b, t, q] = term[
                        t * ROWS : (t + 1) * ROWS, b * LB : (b + 1) * LB
                    ]
        if h == 1:
            pl.semaphore_wait(barrier, len(peers))
            for k in (1, 2, 3):
                go(fsend(k))
            ystart(2)
        else:
            ystart(0)
            ystart(1)
    go(act_copy)
    for s in range(2):
        for lb in (2, 0, 1):
            ystep(lb, s)
    far()
    for lb in (2, 0, 1):
        ystep(lb, 2)
    ystep(3, 0)
    for lb in (2, 0, 1):
        ystep(lb, 3)
        yfinal(lb)
    for s in (1, 2, 3):
        ystep(3, s)
    for c in loads[2:]:
        c.wait()
    for lb in (3, 2, 0, 1):
        adam(lb)
    for i in (O_FIRST, O_SECOND):
        stores[i].start()
        drains.append(stores[i].wait)
    for stage in (owner_a, owner_b, owner_c, wz, wystart):
        for h in range(2):
            stage(h)
    for s in range(4):
        for h in range(2):
            wystep(h, s)
        if s == 1:
            replicated()
    act_copy.wait_recv()
    project(0)
    project(1)
    for h in range(2):
        kcopy(h).wait_recv()
        keys[:, pl.ds(pl.multiple_of((2 * h + 1 - r) * LB, LB), LB)] = krec[h]
    k_store = pltpu.make_async_copy(keys, okeys_hbm, out_sem.at[5])
    k_store.start()
    for drain in drains:
        drain()
    for k in (1, 2):
        tsend(k).wait_send()
    gsend().wait_send()
    for k in (1, 2, 3):
        msend(k).wait_send()

    @pl.when(lax.rem(x, 2) == r)
    def _():
        for k in (1, 2, 3):
            wxsend(0, k).wait_send()

    k_store.wait()


def hand_over(*refs):
    copies = [
        pltpu.make_async_copy(refs[i], refs[6 + i], refs[12].at[i]) for i in range(6)
    ]
    for c in copies:
        c.start()
    for c in copies:
        c.wait()


def body(act, cot, w, m, v, ra, rm, ga, gm):
    dma = pltpu.SemaphoreType.DMA
    flat = lambda a: a.reshape(ROWS, KV)
    out = pl.pallas_call(
        kernel,
        out_shape=[jax.ShapeDtypeStruct((ROWS, KV), F32)] * 5
        + [jax.ShapeDtypeStruct((TOK, KV), BF)],
        in_specs=[pl.BlockSpec(memory_space=pl.ANY)] * 9,
        out_specs=[pl.BlockSpec(memory_space=pl.ANY)] * 6,
        scratch_shapes=[
            pltpu.VMEM((2, TOK, DW), BF),
            pltpu.VMEM((TOK, KV), BF),
            pltpu.VMEM((7, ROWS, KV), F32),
            pltpu.VMEM((4, N_Y, N_ZL, ROWS, LB), BF),
            pltpu.VMEM((2, 3, 4, N_ZL, ROWS, LB), BF),
            pltpu.VMEM((3, N_ZL, ROWS, LB), BF),
            pltpu.VMEM((3, N_ZL, ROWS, LB), BF),
            pltpu.VMEM((3, N_Y, ROWS, LB), BF),
            pltpu.VMEM((N_Y, ROWS, LB), BF),
            pltpu.VMEM((2, 4, ROWS, LB), BF),
            pltpu.VMEM((4, ROWS, LB), BF),
            pltpu.VMEM((N_X, ROWS, LB), BF),
            pltpu.VMEM((N_ZH, ROWS, LB), F32),
            pltpu.VMEM((2, ROWS, LB), F32),
            pltpu.VMEM((N_X, 2, ROWS, LB), F32),
            pltpu.VMEM((2, N_ZL, N_Y, ROWS, LB), BF),
            pltpu.VMEM((2, TOK, LB), BF),
            pltpu.VMEM((2, TOK, LB), BF),
            pltpu.VMEM((5, ROWS, KV), F32),
            pltpu.VMEM((TOK, KV), BF),
            dma((9,)),
            dma((6,)),
            dma((2,)),
            dma((2, 4, 4)),
            dma((2, 4, 4)),
            dma((3, 3)),
            dma((3, 3)),
            dma((3,)),
            dma((3,)),
            dma((4,)),
            dma((4,)),
            dma((2,)),
            dma((2,)),
            dma((2,)),
            dma((3,)),
            dma((4,)),
            dma((3,)),
            dma((2,)),
            dma((2, 3)),
            dma((2, 3)),
            dma((2, 2, 4)),
            dma((2, 2, 4)),
            dma((4,)),
        ],
        compiler_params=pltpu.CompilerParams(
            collective_id=0, has_side_effects=True, vmem_limit_bytes=60 * 1024 * 1024
        ),
        name="outer_sync",
    )(act, cot, *map(flat, (w, m, v, ra, rm, ga, gm)))
    first, second, rv, gv, gn, keys = pl.pallas_call(
        hand_over,
        out_shape=[jax.ShapeDtypeStruct(o.shape, o.dtype) for o in out],
        in_specs=[pl.BlockSpec(memory_space=pltpu.VMEM)] * 6,
        out_specs=[pl.BlockSpec(memory_space=pl.ANY)] * 6,
        scratch_shapes=[dma((6,))],
        name="hand_over",
    )(*out)
    return (
        first.reshape(1, 1, ROWS, KV),
        second.reshape(1, 1, ROWS, KV),
        rv.reshape(1, ROWS, KV),
        gv,
        gn,
        keys,
    )


def solution(mesh):
    finer = Mesh(
        mesh.devices.reshape(2, N_ZH, N_X, N_ZL, N_Y), ("region", "zh", "x", "zl", "y")
    )
    island = ("zh", "x")
    dev = ("zl", "y")
    every = ("region", "zh", "x", "zl", "y")
    return jax.shard_map(
        body,
        mesh=finer,
        in_specs=(
            P(every, None),
            P(every, None),
            P("region", island, dev, None),
            P("region", island, dev, None),
            P("region", island, dev, None),
            P("region", dev, None),
            P("region", dev, None),
            P(dev, None),
            P(dev, None),
        ),
        out_specs=(
            P("region", island, dev, None),
            P("region", island, dev, None),
            P("region", dev, None),
            P(dev, None),
            P(dev, None),
            P(every, None),
        ),
        check_vma=False,
    )
```

time: 288 us -> 90.2 us (0.31)
  waiting for transfers between devices: 182 us -> 0 us
  Pallas kernels: 0 us -> 88.7 us
  blocking collectives: 79.4 us -> 0 us
  between operations: 13.8 us -> 0.64 us
  other arithmetic: 4.97 us -> 0 us
  local copies, waits for them, and re-layouts: 4.14 us -> 0 us
    all_gather x1 -> x0, waiting for transfers between devices: 92.7 us -> none  [over_pieces(): return lax.all_gather(shard, axis).sum(0)]
    reduce_scatter x2 -> x0, waiting for transfers between devices: 88.8 us -> none  [reduced_to_own(): pieces = lax.psum_scatter(pieces, axes[k], scatter_dimension=0, tiled=True)]
    pallas_call x0 -> x2, Pallas kernels: none -> 88.7 us  [the longest x1 86.4 us: body(): pl.pallas_call(kernel, out_shape=[jax.ShapeDtypeStruct((ROWS, KV), F32)]...]
    all_to_all x2 -> x0, blocking collectives: 79.4 us -> none  [copy_for_each(): return lax.all_to_all(copies, axis, split_axis=0, concat_axis=0, tiled=True)]
  transfers between devices with their start and end apart: 3 -> 0, of which waited for: 3 -> 0; matrix products, arithmetic and copies ran while one was open for 0% -> 0% of each run, Pallas kernels for 0% -> 0%
where the time goes in v1:
time: 90.2 us; the launch traced here: 89.4 us
  Pallas kernels  88.7 us (98%)
    pallas_call x1, Pallas kernels, body(): pl.pallas_call(kernel, out_shape=[jax.ShapeDtypeStruct((ROWS, KV), F32)]...  86.4 us
    pallas_call x1, Pallas kernels, body(): pl.pallas_call(hand_over, out_shape=[jax.ShapeDtypeStruct(o.shape, o.dtyp...  2.35 us

profile of v1, /device:TPU:1, one launch (start us, length us, event | category | flops | bytes accessed | tf_op | source)
XLA Modules:
  0.0 89.4 jit_solution(7182717591862682631)
XLA Ops:
  0.6 86.4 %outer_sync.1 = (f32[80,512]{1,0:T(8,128)}, f32[80,512]{1,0:T(8,128)}, f32[80,512]{1,0:T(8,128)}, f32[80,512]{1,0:T(8,128)}, f32[80,512]{1,0:T(8,128)}, /*index=5*/bf16[256,512]{1,0:T(8,128)(2,1)}) custom-call(bf16[256,2560]{1,0:T(8,128)(2,1)} %act_hbm.1, bf16[256,512]{1,0:T(8,128)(2,1)} %cot_hbm.1, f32[80,512]{1,0:T(8,128)} %bitcast.8, f32[80,512]{1,0:T(8,128)} %bitcast.9, ...), custom_call_target="tpu_custom_call" | custom-call | tf_op jit(solution)/shard_map/outer_sync/pallas_call | solution.py:477
  87.0 2.3 %hand_over.1 = (f32[80,512]{1,0:T(8,128)}, f32[80,512]{1,0:T(8,128)}, f32[80,512]{1,0:T(8,128)}, f32[80,512]{1,0:T(8,128)}, f32[80,512]{1,0:T(8,128)}, /*index=5*/bf16[256,512]{1,0:T(8,128)(2,1)}) custom-call(f32[80,512]{1,0:T(8,128)} %get-tuple-element.18.refs_0_, f32[80,512]{1,0:T(8,128)} %get-tuple-element.19.refs_1_, ...), custom_call_target="tpu_custom_call" | custom-call | tf_op jit(solution)/shard_map/hand_over/pallas_call | solution.py:533

commit v2 on v1

--- a/solution.py
+++ b/solution.py
@@ -48,7 +48,8 @@
     gap, means, wfull, ksend, krec, outs, keys,
     in_sem, out_sem, act_sem, ys_sem, yr_sem, zs_sem, zr_sem, fs_sem, fr_sem,
     xs_sem, xr_sem, ts_sem, tr_sem, g_sem, ms_sem, mr_sem, wxs_sem, wxr_sem,
-    wzs_sem, wzr_sem, wys_sem, wyr_sem, k_sem,
+    wz0s_sem, wz0r_sem, wy0s_sem, wy0r_sem, wy1s_sem, wy1r_sem, wz1s_sem, wz1r_sem,
+    k_sem,
 ):
     r = lax.axis_index("region")
     zh = lax.axis_index("zh")
@@ -299,22 +300,7 @@
             for k in (1, 2, 3):
                 msend(k).start()
 
-    def wz_offs(h):
-        return (1, -1, 2 if h == 0 else -2)
-
-    def wzsend(h, i):
-        slot = wfull.at[h, zl, y]
-        return remote(
-            slot, slot, wzs_sem.at[h, i], wzr_sem.at[h, i], to_z(wz_offs(h)[i])
-        )
-
-    def wzrecv(h, i):
-        slot = wfull.at[h, lax.rem(zl - wz_offs(h)[i] + 4, 4), y]
-        return remote(
-            slot, slot, wzs_sem.at[h, i], wzr_sem.at[h, i], to_z(-wz_offs(h)[i])
-        )
-
-    def wz(h):
+    def wx(h):
         @pl.when(x != 2 * h + r)
         def _():
             slot = wfull.at[h, zl, y]
@@ -322,35 +308,89 @@
                 slot, slot, wxs_sem.at[0], wxr_sem.at[h], {"x": 2 * h + r}
             ).wait_recv()
 
+    def near(off):
+        return lax.rem(zl - off + N_ZL, N_ZL)
+
+    def origin(d, s):
+        return lax.rem(y - SIGN[d] * s + N_Y, N_Y)
+
+    offs = (0, 1, -1, 2)
+
+    def z0(j, off):
+        slot = wfull.at[0, near(off), y]
+        return slot, wz0s_sem.at[j - 1], wz0r_sem.at[j - 1]
+
+    def z0send(j):
+        slot, ssem, rsem = z0(j, 0)
+        return remote(slot, slot, ssem, rsem, to_z(offs[j]))
+
+    def z0recv(j):
+        slot, ssem, rsem = z0(j, offs[j])
+        return remote(slot, slot, ssem, rsem, to_z(-offs[j]))
+
+    def y0send(d, j, s):
+        slot = wfull.at[0, near(offs[j]), origin(d, s)]
+        return remote(
+            slot, slot, wy0s_sem.at[d, j, s], wy0r_sem.at[d, j, s], to_y(SIGN[d])
+        )
+
+    def y0recv(d, j, s):
+        slot = wfull.at[0, near(offs[j]), origin(d, s + 1)]
+        return remote(
+            slot, slot, wy0s_sem.at[d, j, s], wy0r_sem.at[d, j, s], to_y(-SIGN[d])
+        )
+
+    def y0start(j):
+        if j > 0:
+            z0recv(j).wait_recv()
+        for d in range(2):
+            go(y0send(d, j, 0))
+
+    def y0step(j, s):
+        for d in range(2):
+            if s < hops(d, j):
+                y0recv(d, j, s).wait_recv()
+                if s + 1 < hops(d, j):
+                    go(y0send(d, j, s + 1))
+
+    def y1(d, s, at):
+        slot = wfull.at[1, zl, origin(d, at)]
+        return slot, slot, wy1s_sem.at[d, s], wy1r_sem.at[d, s]
+
+    def z1off(c, i):
+        return (1, -1, 2 if c % 2 == 0 else -2)[i]
+
+    def z1send(c, at, i):
+        slot = wfull.at[1, zl, at]
+        return remote(
+            slot, slot, wz1s_sem.at[c, i], wz1r_sem.at[c, i], to_z(z1off(c, i))
+        )
+
+    def z1recv(c, at, i):
+        slot = wfull.at[1, near(z1off(c, i)), at]
+        return remote(
+            slot, slot, wz1s_sem.at[c, i], wz1r_sem.at[c, i], to_z(-z1off(c, i))
+        )
+
+    pieces = [(0, y)]
+
+    def y1start():
+        for d in range(2):
+            go(remote(*y1(d, 0, 0), to_y(SIGN[d])))
         for i in range(3):
-            go(wzsend(h, i))
-
-    def wysend(d, h, s):
-        slot = wfull.at[h, :, lax.rem(y - SIGN[d] * s + N_Y, N_Y)]
-        return remote(
-            slot, slot, wys_sem.at[d, h, s], wyr_sem.at[d, h, s], to_y(SIGN[d])
-        )
-
-    def wyrecv(d, h, s):
-        slot = wfull.at[h, :, lax.rem(y - SIGN[d] * (s + 1) + N_Y, N_Y)]
-        return remote(
-            slot, slot, wys_sem.at[d, h, s], wyr_sem.at[d, h, s], to_y(-SIGN[d])
-        )
-
-    def wystart(h):
-        for i in range(3):
-            wzrecv(h, i).wait_recv()
+            go(z1send(0, y, i))
+
+    def y1step(s):
         for d in range(2):
-            go(wysend(d, h, 0))
-
-    def wystep(h, s):
-        for d in range(2):
-            n = hops(d, h)
-            if s >= n:
-                continue
-            wyrecv(d, h, s).wait_recv()
-            if s + 1 < n:
-                go(wysend(d, h, s + 1))
+            n = hops(d, 0)
+            if s < n:
+                remote(*y1(d, s, s + 1), to_y(-SIGN[d])).wait_recv()
+                if s + 1 < n:
+                    go(remote(*y1(d, s + 1, s + 1), to_y(SIGN[d])))
+                c, at = len(pieces), origin(d, s + 1)
+                pieces.append((c, at))
+                for i in (2, 0, 1):
+                    go(z1send(c, at, i))
 
     def replicated():
         for lb in range(4):
@@ -378,15 +418,33 @@
     def kcopy(h):
         return remote(ksend.at[h], krec.at[h], k_sem.at[h], k_sem.at[2 + h], other)
 
-    def project(h):
-        rhs = wfull[h].reshape(DW, LB)
-        ksend[h] = (
-            jnp.dot(act[1], rhs, preferred_element_type=F32) * scale
-        ).astype(BF)
+    def finish(h, theirs, ours):
+        ksend[h] = (theirs * scale).astype(BF)
         go(kcopy(h))
         keys[:, pl.ds(pl.multiple_of((2 * h + r) * LB, LB), LB)] = (
-            jnp.dot(act[0], rhs, preferred_element_type=F32) * scale
+            ours * scale
         ).astype(BF)
+
+    def project0():
+        rhs = wfull[0].reshape(DW, LB)
+        finish(
+            0,
+            jnp.dot(act[1], rhs, preferred_element_type=F32),
+            jnp.dot(act[0], rhs, preferred_element_type=F32),
+        )
+
+    def project1():
+        theirs = ours = 0.0
+        for i in (None, 0, 1, 2):
+            if i is not None:
+                for c, at in pieces:
+                    z1recv(c, at, i).wait_recv()
+            q = near((0, 1, -1, 2)[0 if i is None else i + 1])
+            rhs = wfull[1, q].reshape(640, LB)
+            span = pl.ds(pl.multiple_of(q * 640, LB), 640)
+            theirs += jnp.dot(act[1, :, span], rhs, preferred_element_type=F32)
+            ours += jnp.dot(act[0, :, span], rhs, preferred_element_type=F32)
+        finish(1, theirs, ours)
 
     act_copy = remote(act.at[0], act.at[1], act_sem.at[0], act_sem.at[1], other)
     for h in (1, 0):
@@ -420,26 +478,44 @@
     for lb in (2, 0, 1):
         ystep(lb, 3)
         yfinal(lb)
-    for s in (1, 2, 3):
-        ystep(3, s)
     for c in loads[2:]:
         c.wait()
-    for lb in (3, 2, 0, 1):
-        adam(lb)
+    ystep(3, 1)
+    adam(2)
+    ystep(3, 2)
+    adam(0)
+    adam(1)
+    ystep(3, 3)
+    adam(3)
     for i in (O_FIRST, O_SECOND):
         stores[i].start()
         drains.append(stores[i].wait)
-    for stage in (owner_a, owner_b, owner_c, wz, wystart):
+    for stage in (owner_a, owner_b, owner_c):
         for h in range(2):
             stage(h)
-    for s in range(4):
-        for h in range(2):
-            wystep(h, s)
-        if s == 1:
-            replicated()
+    wx(0)
+    for j in (1, 2, 3):
+        go(z0send(j))
+    y0start(0)
+    wx(1)
+    y1start()
+    y1step(0)
+    y0step(0, 0)
+    for j in (1, 2, 3):
+        y0start(j)
+    y1step(1)
+    for s in range(3):
+        y0step(0, s + 1)
+        for j in (1, 2, 3):
+            y0step(j, s)
+        if s < 2:
+            y1step(s + 2)
+    replicated()
+    for j in (1, 2, 3):
+        y0step(j, 3)
     act_copy.wait_recv()
-    project(0)
-    project(1)
+    project0()
+    project1()
     for h in range(2):
         kcopy(h).wait_recv()
         keys[:, pl.ds(pl.multiple_of((2 * h + 1 - r) * LB, LB), LB)] = krec[h]
@@ -462,13 +538,20 @@
 
 
 def hand_over(*refs):
-    copies = [
-        pltpu.make_async_copy(refs[i], refs[6 + i], refs[12].at[i]) for i in range(6)
+    sem = refs[18]
+    loads = [
+        pltpu.make_async_copy(refs[i], refs[12 + i], sem.at[0, i]) for i in range(6)
     ]
-    for c in copies:
+    stores = [
+        pltpu.make_async_copy(refs[12 + i], refs[6 + i], sem.at[1, i]) for i in range(6)
+    ]
+    for c in loads:
         c.start()
-    for c in copies:
+    for c, o in zip(loads, stores):
         c.wait()
+        o.start()
+    for o in stores:
+        o.wait()
 
 
 def body(act, cot, w, m, v, ra, rm, ga, gm):
@@ -519,10 +602,14 @@
             dma((4,)),
             dma((3,)),
             dma((2,)),
-            dma((2, 3)),
-            dma((2, 3)),
-            dma((2, 2, 4)),
-            dma((2, 2, 4)),
+            dma((3,)),
+            dma((3,)),
+            dma((2, 4, 4)),
+            dma((2, 4, 4)),
+            dma((2, 4)),
+            dma((2, 4)),
+            dma((8, 3)),
+            dma((8, 3)),
             dma((4,)),
         ],
         compiler_params=pltpu.CompilerParams(
@@ -533,9 +620,10 @@
     first, second, rv, gv, gn, keys = pl.pallas_call(
         hand_over,
         out_shape=[jax.ShapeDtypeStruct(o.shape, o.dtype) for o in out],
-        in_specs=[pl.BlockSpec(memory_space=pltpu.VMEM)] * 6,
+        in_specs=[pl.BlockSpec(memory_space=pl.ANY)] * 6,
         out_specs=[pl.BlockSpec(memory_space=pl.ANY)] * 6,
-        scratch_shapes=[dma((6,))],
+        scratch_shapes=[pltpu.VMEM(o.shape, o.dtype) for o in out] + [dma((2, 6))],
+        compiler_params=pltpu.CompilerParams(vmem_limit_bytes=60 * 1024 * 1024),
         name="hand_over",
     )(*out)
     return (

time: 90.2 us -> 83.6 us (0.927)
  Pallas kernels: 88.7 us -> 82.8 us
    pallas_call x1, Pallas kernels: 86.4 us -> 80.6 us  [body(): pl.pallas_call(kernel, out_shape=[jax.ShapeDtypeStruct((ROWS, KV), F32)]...]
where the time goes in v2:
time: 83.6 us; the launch traced here: 83.4 us
  Pallas kernels  82.8 us (99%)
    pallas_call x1, Pallas kernels, body(): pl.pallas_call(kernel, out_shape=[jax.ShapeDtypeStruct((ROWS, KV), F32)]...  80.6 us
    pallas_call x1, Pallas kernels, body(): pl.pallas_call(hand_over, out_shape=[jax.ShapeDtypeStruct(o.shape, o.dtyp...  2.13 us

profile of v2, /device:TPU:1, one launch (start us, length us, event | category | flops | bytes accessed | tf_op | source)
XLA Modules:
  0.0 83.4 jit_solution(15993793737389568417)
XLA Ops:
  0.6 80.6 %outer_sync.1 = (f32[80,512]{1,0:T(8,128)}, f32[80,512]{1,0:T(8,128)}, f32[80,512]{1,0:T(8,128)}, f32[80,512]{1,0:T(8,128)}, f32[80,512]{1,0:T(8,128)}, /*index=5*/bf16[256,512]{1,0:T(8,128)(2,1)}) custom-call(bf16[256,2560]{1,0:T(8,128)(2,1)} %act_hbm.1, bf16[256,512]{1,0:T(8,128)(2,1)} %cot_hbm.1, f32[80,512]{1,0:T(8,128)} %bitcast.8, f32[80,512]{1,0:T(8,128)} %bitcast.9, ...), custom_call_target="tpu_custom_call" | custom-call | tf_op jit(solution)/shard_map/outer_sync/pallas_call | solution.py:560
  81.3 2.1 %hand_over.1 = (f32[80,512]{1,0:T(8,128)}, f32[80,512]{1,0:T(8,128)}, f32[80,512]{1,0:T(8,128)}, f32[80,512]{1,0:T(8,128)}, f32[80,512]{1,0:T(8,128)}, /*index=5*/bf16[256,512]{1,0:T(8,128)(2,1)}) custom-call(f32[80,512]{1,0:T(8,128)} %get-tuple-element.18.refs_0_, f32[80,512]{1,0:T(8,128)} %get-tuple-element.19.refs_1_, ...), custom_call_target="tpu_custom_call" | custom-call | tf_op jit(solution)/shard_map/hand_over/pallas_call | solution.py:620

commit v3 on v2

--- a/solution.py
+++ b/solution.py
@@ -297,8 +297,6 @@
                     wxsend(h, k).start()
 
             means[x, 1] = global_mean
-            for k in (1, 2, 3):
-                msend(k).start()
 
     def wx(h):
         @pl.when(x != 2 * h + r)
@@ -425,26 +423,29 @@
             ours * scale
         ).astype(BF)
 
-    def project0():
-        rhs = wfull[0].reshape(DW, LB)
-        finish(
-            0,
-            jnp.dot(act[1], rhs, preferred_element_type=F32),
-            jnp.dot(act[0], rhs, preferred_element_type=F32),
-        )
-
-    def project1():
-        theirs = ours = 0.0
-        for i in (None, 0, 1, 2):
-            if i is not None:
-                for c, at in pieces:
-                    z1recv(c, at, i).wait_recv()
-            q = near((0, 1, -1, 2)[0 if i is None else i + 1])
-            rhs = wfull[1, q].reshape(640, LB)
-            span = pl.ds(pl.multiple_of(q * 640, LB), 640)
-            theirs += jnp.dot(act[1, :, span], rhs, preferred_element_type=F32)
-            ours += jnp.dot(act[0, :, span], rhs, preferred_element_type=F32)
-        finish(1, theirs, ours)
+    def slab(h, j):
+        q = near(offs[j])
+        rhs = wfull[h, q].reshape(640, LB)
+        span = pl.ds(pl.multiple_of(q * 640, LB), 640)
+        return (
+            jnp.dot(act[1, :, span], rhs, preferred_element_type=F32),
+            jnp.dot(act[0, :, span], rhs, preferred_element_type=F32),
+        )
+
+    def project(h, ready):
+        theirs, ours = slab(h, 0)
+        for j in (1, 2, 3):
+            ready(j)
+            more = slab(h, j)
+            theirs, ours = theirs + more[0], ours + more[1]
+        finish(h, theirs, ours)
+
+    def ready0(j):
+        y0step(j, 3)
+
+    def ready1(j):
+        for c, at in pieces:
+            z1recv(c, at, j - 1).wait_recv()
 
     act_copy = remote(act.at[0], act.at[1], act_sem.at[0], act_sem.at[1], other)
     for h in (1, 0):
@@ -499,6 +500,8 @@
     y0start(0)
     wx(1)
     y1start()
+    for k in (1, 2, 3):
+        msend(k).start()
     y1step(0)
     y0step(0, 0)
     for j in (1, 2, 3):
@@ -511,12 +514,10 @@
         if s < 2:
             y1step(s + 2)
     replicated()
-    for j in (1, 2, 3):
-        y0step(j, 3)
     act_copy.wait_recv()
-    project0()
-    project1()
-    for h in range(2):
+    project(1, ready1)
+    project(0, ready0)
+    for h in (1, 0):
         kcopy(h).wait_recv()
         keys[:, pl.ds(pl.multiple_of((2 * h + 1 - r) * LB, LB), LB)] = krec[h]
     k_store = pltpu.make_async_copy(keys, okeys_hbm, out_sem.at[5])

time: 83.6 us -> 83.6 us (level)
  no operation moved by 1% of the time
where the time goes in v3:
time: 83.6 us; the launch traced here: 83.4 us
  Pallas kernels  82.7 us (99%)
    pallas_call x1, Pallas kernels, body(): pl.pallas_call(kernel, out_shape=[jax.ShapeDtypeStruct((ROWS, KV), F32)]...  80.6 us
    pallas_call x1, Pallas kernels, body(): pl.pallas_call(hand_over, out_shape=[jax.ShapeDtypeStruct(o.shape, o.dtyp...  2.13 us

profile of v3, /device:TPU:1, one launch (start us, length us, event | category | flops | bytes accessed | tf_op | source)
XLA Modules:
  0.0 83.4 jit_solution(2060728140908758380)
XLA Ops:
  0.6 80.6 %outer_sync.1 = (f32[80,512]{1,0:T(8,128)}, f32[80,512]{1,0:T(8,128)}, f32[80,512]{1,0:T(8,128)}, f32[80,512]{1,0:T(8,128)}, f32[80,512]{1,0:T(8,128)}, /*index=5*/bf16[256,512]{1,0:T(8,128)(2,1)}) custom-call(bf16[256,2560]{1,0:T(8,128)(2,1)} %act_hbm.1, bf16[256,512]{1,0:T(8,128)(2,1)} %cot_hbm.1, f32[80,512]{1,0:T(8,128)} %bitcast.8, f32[80,512]{1,0:T(8,128)} %bitcast.9, ...), custom_call_target="tpu_custom_call" | custom-call | tf_op jit(solution)/shard_map/outer_sync/pallas_call | solution.py:561
  81.2 2.1 %hand_over.1 = (f32[80,512]{1,0:T(8,128)}, f32[80,512]{1,0:T(8,128)}, f32[80,512]{1,0:T(8,128)}, f32[80,512]{1,0:T(8,128)}, f32[80,512]{1,0:T(8,128)}, /*index=5*/bf16[256,512]{1,0:T(8,128)(2,1)}) custom-call(f32[80,512]{1,0:T(8,128)} %get-tuple-element.18.refs_0_, f32[80,512]{1,0:T(8,128)} %get-tuple-element.19.refs_1_, ...), custom_call_target="tpu_custom_call" | custom-call | tf_op jit(solution)/shard_map/hand_over/pallas_call | solution.py:621

commit v4 on v3

--- a/solution.py
+++ b/solution.py
@@ -221,7 +221,7 @@
         )
         outs[O_FIRST, :, lanes] = first
         outs[O_SECOND, :, lanes] = second
-        delta[lb] = (state[RA, :, lanes] - inner).astype(BF)
+        delta[lb] = state[RA, :, lanes] - inner
         go_if(x != lb, lambda: xsend(lb))
 
     mine = pl.ds(pl.multiple_of(x * LB, LB), LB)
@@ -244,14 +244,14 @@
     def owner_a(h):
         @pl.when(x // 2 == h)
         def _():
-            t = delta[x].astype(F32)
+            t = delta[x]
             for k in (1, 2, 3):
                 src = lax.rem(x + k, N_X)
                 remote(
                     delta.at[0], xrec.at[src], xs_sem.at[0], xr_sem.at[src], {"x": src}
                 ).wait_recv()
-                t = t + xrec[src].astype(F32)
-            trec[zh] = t
+                t = t + xrec[src]
+            trec[zh] = t.astype(BF)
             for k in (1, 2):
                 tsend(k).start()
 
@@ -260,7 +260,9 @@
         def _():
             for k in (1, 2):
                 trecv(k).wait_recv()
-            region_mean = ((trec[0] + trec[1]) + trec[2]) / 12
+            region_mean = (
+                (trec[0].astype(F32) + trec[1].astype(F32)) + trec[2].astype(F32)
+            ) / 12
             region_velocity = region_mu * state[RM, :, mine] + region_mean
             region_params = state[RA, :, mine] - region_rate * (
                 region_mean + region_mu * region_velocity
@@ -297,6 +299,8 @@
                     wxsend(h, k).start()
 
             means[x, 1] = global_mean
+            for k in (1, 2, 3):
+                msend(k).start()
 
     def wx(h):
         @pl.when(x != 2 * h + r)
@@ -500,8 +504,6 @@
     y0start(0)
     wx(1)
     y1start()
-    for k in (1, 2, 3):
-        msend(k).start()
     y1step(0)
     y0step(0, 0)
     for j in (1, 2, 3):
@@ -575,9 +577,9 @@
             pltpu.VMEM((3, N_Y, ROWS, LB), BF),
             pltpu.VMEM((N_Y, ROWS, LB), BF),
             pltpu.VMEM((2, 4, ROWS, LB), BF),
-            pltpu.VMEM((4, ROWS, LB), BF),
-            pltpu.VMEM((N_X, ROWS, LB), BF),
-            pltpu.VMEM((N_ZH, ROWS, LB), F32),
+            pltpu.VMEM((4, ROWS, LB), F32),
+            pltpu.VMEM((N_X, ROWS, LB), F32),
+            pltpu.VMEM((N_ZH, ROWS, LB), BF),
             pltpu.VMEM((2, ROWS, LB), F32),
             pltpu.VMEM((N_X, 2, ROWS, LB), F32),
             pltpu.VMEM((2, N_ZL, N_Y, ROWS, LB), BF),

time: 83.6 us -> 82.7 us (0.989)
    pallas_call x1, Pallas kernels: 80.6 us -> 79.7 us  [body(): pl.pallas_call(kernel, out_shape=[jax.ShapeDtypeStruct((ROWS, KV), F32)]...]
where the time goes in v4:
time: 82.7 us; the launch traced here: 82.5 us
  Pallas kernels  81.9 us (99%)
    pallas_call x1, Pallas kernels, body(): pl.pallas_call(kernel, out_shape=[jax.ShapeDtypeStruct((ROWS, KV), F32)]...  79.7 us
    pallas_call x1, Pallas kernels, body(): pl.pallas_call(hand_over, out_shape=[jax.ShapeDtypeStruct(o.shape, o.dtyp...  2.13 us

profile of v4, /device:TPU:1, one launch (start us, length us, event | category | flops | bytes accessed | tf_op | source)
XLA Modules:
  0.0 82.5 jit_solution(14629901829529976697)
XLA Ops:
  0.6 79.7 %outer_sync.1 = (f32[80,512]{1,0:T(8,128)}, f32[80,512]{1,0:T(8,128)}, f32[80,512]{1,0:T(8,128)}, f32[80,512]{1,0:T(8,128)}, f32[80,512]{1,0:T(8,128)}, /*index=5*/bf16[256,512]{1,0:T(8,128)(2,1)}) custom-call(bf16[256,2560]{1,0:T(8,128)(2,1)} %act_hbm.1, bf16[256,512]{1,0:T(8,128)(2,1)} %cot_hbm.1, f32[80,512]{1,0:T(8,128)} %bitcast.8, f32[80,512]{1,0:T(8,128)} %bitcast.9, ...), custom_call_target="tpu_custom_call" | custom-call | tf_op jit(solution)/shard_map/outer_sync/pallas_call | solution.py:563
  80.4 2.1 %hand_over.1 = (f32[80,512]{1,0:T(8,128)}, f32[80,512]{1,0:T(8,128)}, f32[80,512]{1,0:T(8,128)}, f32[80,512]{1,0:T(8,128)}, f32[80,512]{1,0:T(8,128)}, /*index=5*/bf16[256,512]{1,0:T(8,128)(2,1)}) custom-call(f32[80,512]{1,0:T(8,128)} %get-tuple-element.18.refs_0_, f32[80,512]{1,0:T(8,128)} %get-tuple-element.19.refs_1_, ...), custom_call_target="tpu_custom_call" | custom-call | tf_op jit(solution)/shard_map/hand_over/pallas_call | solution.py:623
